TPU v7x, 512 devices: a whole 4x4x16 slice. The times are simulated.
512 devices in a mesh: section: 8 (over x, z_hi), ctx: 32 (over z_lo, y), tp: 2 (over core).
Axes of the slice: x: 4, y: 4, z: 16 (z_hi: 2, z_lo: 8; z = z_hi * 8 + z_lo), core: 2. Of those that a mesh axis runs over, the one named last changes fastest.
Arguments:
- queries: bfloat16 [8, 2, 4096, 4096], P('section', None, 'ctx', 'tp'), may hold values from -48 to 48
- keyvals: bfloat16 [8, 2, 2, 4096, 512], P('section', None, None, ('ctx', 'tp')), may hold values from -4 to 4
- segments: int32 [8, 2, 4096], P('section', None, 'ctx'), may hold values from 0 to 3, never falling along the last dimension, each value on 1 to 3072 neighbouring positions
Outputs:
- handed: bfloat16 [8, 2, 4096, 4096], P('section', None, 'ctx', 'tp')
Inputs may be any that keep to these rules, and one draw needn't show every extreme that they name: `segments`: document numbers never fall along a stream; each document is at most 3072 positions long, and one is exactly that long.
All inputs are finite; a program needn't handle non-finite values.
Results may differ from a plain program's by a relative error of at most 0.0035.
Values may be sent and summed in bfloat16 or wider, within the bound.
No kernel may reach another device: no remote copies, remote signals or barrier semaphores. Data moves between devices by JAX's collectives and lax.ppermute only.
A program may use at most 128 MiB of HBM per device.

v0:
```python
import math
import jax
import jax.numpy as jnp
from jax import lax
from jax.sharding import PartitionSpec as P

HEADS = 32
KVH = 4
HD = 128


def from_behind(block, axis, distance):
    devices = range(lax.axis_size(axis))
    route = [(i - distance, i) for i in devices if i - distance in devices]
    return lax.ppermute(block, axis, route)


def attend_piece(
    carry_state, key_value, key_docs, first, query_heads, query_docs, query_pos, query_end
):
    key_count = key_value.shape[1]
    block_len = math.gcd(key_count, 512)
    scale = 1.0 / math.sqrt(HD)

    def sweep_keys(state_in):

        def one_block(step_num, state_now):
            row_max, row_sum, out_sum = state_now
            offset = step_num * block_len
            slab_piece = lax.dynamic_slice_in_dim(key_value, offset, block_len, 1)
            key_rows = slab_piece[0].reshape(block_len, -1, HD)
            value_rows = slab_piece[1].reshape(block_len, -1, HD)
            block_docs = lax.dynamic_slice_in_dim(key_docs, offset, block_len, 0)
            key_pos = offset + jnp.arange(block_len, dtype=jnp.int32)
            allowed = (query_docs[:, None] == block_docs[None, :]) & (
                key_pos[None, :] <= query_pos[:, None]
            )
            allowed = allowed[:, None, None, :]
            scores = (
                jnp.einsum(
                    "tgjd,ngd->tgjn", query_heads, key_rows, preferred_element_type=jnp.float32
                )
                * scale
            )
            scores = jnp.where(allowed, scores, -1e30)
            new_max = jnp.maximum(row_max, jnp.max(scores, axis=-1))
            exp_terms = jnp.where(allowed, jnp.exp(scores - new_max[..., None]), 0.0)
            factor = jnp.exp(row_max - new_max)
            row_sum = factor * row_sum + jnp.sum(exp_terms, axis=-1)
            weights = exp_terms.astype(jnp.bfloat16)
            out_sum = factor[..., None] * out_sum + jnp.einsum(
                "tgjn,ngd->tgjd", weights, value_rows, preferred_element_type=jnp.float32
            )
            return (new_max, row_sum, out_sum)

        return lax.fori_loop(0, key_count // block_len, one_block, state_in)

    is_live = (first < query_end) & (key_docs[key_count - 1] >= query_docs[0])
    return lax.cond(is_live, sweep_keys, lambda state_same: state_same, carry_state)


def make_fold(streams, query_list, doc_list, query_pos, query_end):

    def fold_piece(carries, shard_piece, first):
        piece_kv, piece_docs = shard_piece
        stream_num = streams[0]
        key_value = piece_kv[0]
        updated = [
            attend_piece(
                carries[0],
                key_value,
                piece_docs[0, 0],
                first,
                query_list[stream_num],
                doc_list[stream_num],
                query_pos,
                query_end,
            )
        ]
        return tuple(updated)

    return fold_piece


def local(queries, keyvals, segments):
    tokens = queries.shape[2]
    groups = HEADS // KVH
    tp_count = lax.axis_size("tp")
    local_heads = KVH // tp_count
    query_start = lax.axis_index("ctx") * tokens
    query_pos = query_start + jnp.arange(tokens, dtype=jnp.int32)
    query_end = query_start + tokens
    query_list = [
        queries[0, stream_num].reshape(tokens, local_heads, groups, HD) for stream_num in range(2)
    ]
    doc_list = [segments[0, stream_num] for stream_num in range(2)]
    head_major = lax.all_to_all(keyvals[0], "tp", split_axis=3, concat_axis=2, tiled=True)
    key_docs = segments[0][:, None, :]
    finals = []
    for stream_num in range(2):
        fold_piece = make_fold([stream_num], query_list, doc_list, query_pos, query_end)
        result = fold_piece(
            (
                (
                    jnp.full((tokens, local_heads, groups), -1e30, jnp.float32),
                    jnp.zeros((tokens, local_heads, groups), jnp.float32),
                    jnp.zeros((tokens, local_heads, groups, HD), jnp.float32),
                ),
            ),
            (
                lax.all_gather(head_major[stream_num : stream_num + 1], "ctx", axis=2, tiled=True),
                lax.all_gather(key_docs[stream_num : stream_num + 1], "ctx", axis=2, tiled=True),
            ),
            jnp.int32(0),
        )
        finals.append(result[0])
    attended = []
    for final_state in finals:
        row_max, row_sum, out_sum = final_state
        attended.append(
            (out_sum / row_sum[..., None])
            .reshape(tokens, local_heads * groups * HD)
            .astype(jnp.bfloat16)
        )
    sent_down = from_behind(attended[0], "section", 1)
    sent_up = from_behind(attended[1], "section", -1)
    section_index = lax.axis_index("section")
    section_last = lax.axis_size("section") - 1
    down_side = jnp.where(section_index == 0, attended[1], sent_down)
    up_side = jnp.where(section_index == section_last, attended[0], sent_up)
    return jnp.stack([down_side, up_side], axis=0)[None]


def solution(mesh):
    return jax.shard_map(
        local,
        mesh=mesh,
        in_specs=(
            P("section", None, "ctx", "tp"),
            P("section", None, None, ("ctx", "tp"), None),
            P("section", None, "ctx"),
        ),
        out_specs=P("section", None, "ctx", "tp"),
        check_vma=False,
    )
```

profile of v0, /device:TPU:2, one launch (start us, length us, event | category | flops | bytes accessed | tf_op | source)
XLA Modules:
  0.0 629.4 jit_solution(5232392392438107751)
XLA Ops:
  6.5 1.3 copy.41
  8.7 3.9 all_to_all.15
  15.4 124.5 %all_gather.14 = s32[1,1,4096]{2,1,0:T(1,128)S(1)} all-gather(s32[1,1,128]{2,1,0:T(1,128)S(1)} %get-tuple-element.558), channel_id=1, replica_groups=mesh['section'=8,'ctx'=32,'tp'=2] {'ctx'}, dimensions={2}, use_global_device_ids=true | all-gather | bytes 16896 | tf_op jit(solution)/shard_map/all_gather | solution.py:112
  142.3 105.1 %all-gather.5.cloned.1.call-done = bf16[1,2,4096,256]{3,2,1,0:T(8,128)(2,1)} async-done(((bf16[1,2,128,256]{3,2,1,0:T(8,128)(2,1)}), bf16[1,2,4096,256]{3,2,1,0:T(8,128)(2,1)}) %all-gather.5.cloned.1.call-update) | async-done | bytes 4194320 | tf_op jit(solution)/shard_map/all_gather | solution.py:111
  247.4 103.2 %conditional.3 = (f32[128,2,8]{0,2,1:T(8,128)}, f32[128,2,8,128]{0,3,2,1:T(8,128)}) conditional(s32[]{:T(128)} %convert_element_type.35, () %tuple.51, (bf16[1,2,4096,256]{3,2,1,0:T(8,128)(2,1)}, s32[1,1,4096]{2,1,0:T(1,128)S(1)}, bf16[1,2,128,2048]{3,2,1,0:T(8,128)(2,1)S(1)}, s32[1,1,128]{2,1,0:T(1,128)S(1)}, s32[128]{0:T(128)S(1)}) %tuple.126), branch_computations={%region_6.7_spmd, %region_7.12_spmd} | conditional | flops 551496192 | bytes 46542204 | solution.py:59
  247.4 6.3 %copy.48 = bf16[1,2,4096,256]{2,3,1,0:T(8,128)(2,1)} copy(bf16[1,2,4096,256]{3,2,1,0:T(8,128)(2,1)} %get-tuple-element.500) | data formatting | bytes 8388608 | tf_op jit(solution)/shard_map
  254.8 95.8 %while.35 = (s32[]{:T(128)}, f32[128,2,8]{0,2,1:T(8,128)S(1)}, f32[128,2,8]{0,2,1:T(8,128)}, f32[128,2,8,128]{0,3,2,1:T(8,128)}, s32[1,1,128]{2,1,0:T(1,128)S(1)...) while((s32[]{:T(128)}, f32[128,2,8]{0,2,1:T(8,128)S(1)}, ...), condition=%wide.region_11.11_spmd.clone, body=%wide.region_8.10_spmd.clone.sunk | while | flops 551496192 | bytes 33959156 | solution.py:56
  256.1 2.8 fusion.61
  258.9 3.3 fusion.62
  262.9 2.2 fusion.64
  266.4 2.8 fusion.61
  269.2 3.3 fusion.62
  273.9 3.4 fusion.64
  278.6 2.8 fusion.61
  281.4 3.3 fusion.62
  286.1 3.4 fusion.64
  290.8 2.8 fusion.61
  293.6 3.4 fusion.62
  298.3 3.4 fusion.64
  303.1 2.8 fusion.61
  305.9 3.3 fusion.62
  310.5 3.4 fusion.64
  315.3 2.8 fusion.61
  318.1 3.3 fusion.62
  322.7 3.4 fusion.64
  327.5 2.8 fusion.61
  330.3 3.3 fusion.62
  334.9 3.4 fusion.64
  339.7 2.8 fusion.61
  342.5 3.3 fusion.62
  347.1 3.4 fusion.64
  350.6 1.3 divide_convert_fusion
  352.1 11.6 %collective-permute-start = (bf16[128,2048]{1,0:T(8,128)(2,1)S(1)}, bf16[128,2048]{1,0:T(8,128)(2,1)}, u32[]{:S(2)}, u32[]{:S(2)}) collective-permute-start(bf16[128,2048]{1,0:T(8,128)(2,1)S(1)} %copy.59), channel_id=1, source_target_pairs={{0,64},{64,128},{128,192},{192,256},{256,320},{320,384},{384,448},... | collective-permute-start | bytes 1572872 | tf_op jit(solution)/shard_map/ppermute | solution.py:15
  363.7 116.3 %all_gather.12 = s32[1,1,4096]{2,1,0:T(1,128)S(1)} all-gather(s32[1,1,128]{2,1,0:T(1,128)S(1)} %get-tuple-element.557), channel_id=1, replica_groups=mesh['section'=8,'ctx'=32,'tp'=2] {'ctx'}, dimensions={2}, use_global_device_ids=true | all-gather | bytes 16896 | tf_op jit(solution)/shard_map/all_gather | solution.py:112
  481.9 14.7 %all-gather.3.cloned.1.call-done = bf16[1,2,4096,256]{3,2,1,0:T(8,128)(2,1)} async-done(((bf16[1,2,128,256]{3,2,1,0:T(8,128)(2,1)}), bf16[1,2,4096,256]{3,2,1,0:T(8,128)(2,1)}) %all-gather.3.cloned.1.call-update) | async-done | bytes 4194320 | tf_op jit(solution)/shard_map/all_gather | solution.py:111
  496.6 103.5 %conditional.2 = (f32[128,2,8]{0,2,1:T(8,128)}, f32[128,2,8,128]{0,3,2,1:T(8,128)}) conditional(s32[]{:T(128)} %convert_element_type.32, () %tuple.49, (bf16[1,2,4096,256]{3,2,1,0:T(8,128)(2,1)}, s32[1,1,4096]{2,1,0:T(1,128)S(1)}, bf16[1,2,128,2048]{3,2,1,0:T(8,128)(2,1)S(1)}, s32[1,1,128]{2,1,0:T(1,128)S(1)}, s32[128]{0:T(128)S(1)}) %tuple.127), branch_computations={%region_0.0_spmd, %region_1.6_spmd} | conditional | flops 551496192 | bytes 46542204 | solution.py:59
  496.6 6.5 %copy.44 = bf16[1,2,4096,256]{2,3,1,0:T(8,128)(2,1)} copy(bf16[1,2,4096,256]{3,2,1,0:T(8,128)(2,1)} %get-tuple-element.495) | data formatting | bytes 8388608 | tf_op jit(solution)/shard_map
  504.1 96.0 %while.34 = (s32[]{:T(128)}, f32[128,2,8]{0,2,1:T(8,128)S(1)}, f32[128,2,8]{0,2,1:T(8,128)}, f32[128,2,8,128]{0,3,2,1:T(8,128)}, s32[1,1,128]{2,1,0:T(1,128)S(1)...) while((s32[]{:T(128)}, f32[128,2,8]{0,2,1:T(8,128)S(1)}, ...), condition=%wide.region_5.5_spmd.clone, body=%wide.region_2.4_spmd.clone.sunk | while | flops 551496192 | bytes 33959156 | solution.py:56
  505.5 2.8 fusion.69
  508.3 3.3 fusion.70
  512.2 2.2 fusion.72
  515.8 2.8 fusion.69
  518.6 3.3 fusion.70
  523.2 3.4 fusion.72
  528.0 2.8 fusion.69
  530.8 3.3 fusion.70
  535.5 3.4 fusion.72
  540.3 2.8 fusion.69
  543.1 3.3 fusion.70
  547.7 3.4 fusion.72
  552.5 2.8 fusion.69
  555.3 3.3 fusion.70
  560.0 3.4 fusion.72
  564.8 2.8 fusion.69
  567.6 3.3 fusion.70
  572.2 3.4 fusion.72
  577.0 2.8 fusion.69
  579.8 3.3 fusion.70
  584.4 3.4 fusion.72
  589.2 2.8 fusion.69
  592.0 3.3 fusion.70
  596.7 3.4 fusion.72
  601.7 5.1 collective-permute-start.1
  607.9 13.5 %collective-permute-done.1 = bf16[128,2048]{1,0:T(8,128)(2,1)S(1)} collective-permute-done((bf16[128,2048]{1,0:T(8,128)(2,1)S(1)}, bf16[128,2048]{1,0:T(8,128)(2,1)S(1)}, u32[]{:S(2)}, u32[]{:S(2)}) %collective-permute-start.1) | collective-permute-done | bytes 524320 | tf_op jit(solution)/shard_map/ppermute | solution.py:15
  (183 shorter events, 52.6 us)
Async XLA Ops:
  6.5 8.8 %copy-start.3 = (s32[1,2,128]{2,1,0:T(2,128)S(1)}, s32[1,2,128]{2,1,0:T(2,128)}, u32[]{:S(2)}) copy-start(s32[1,2,128]{2,1,0:T(2,128)} %param.13) | copy-start | bytes 3076
  6.5 240.9 %copy-start.2 = (bf16[1,2,128,2048]{3,2,1,0:T(8,128)(2,1)S(1)}, bf16[1,2,128,2048]{3,2,1,0:T(8,128)(2,1)}, u32[]{:S(2)}) copy-start(bf16[1,2,128,2048]{3,2,1,0:T(8,128)(2,1)} %param.11) | copy-start | bytes 3145732
  6.5 240.9 %all-gather.5.cloned.1.call-start = ((), (), s32[]{:S(2)}) async-start(), calls=%async_computation.2 | async-start | bytes 4325376 | tf_op jit(solution)/shard_map/all_gather | solution.py:111
  14.6 481.9 %all-gather.3.cloned.1.call-start = ((), (), s32[]{:S(2)}) async-start(), calls=%async_computation.1 | async-start | bytes 4325376 | tf_op jit(solution)/shard_map/all_gather | solution.py:111
  258.9 4.0 copy-start
  269.2 4.7 copy-start
  281.4 4.7 copy-start
  293.6 4.7 copy-start
  305.9 4.7 copy-start
  318.1 4.7 copy-start
  330.3 4.7 copy-start
  342.5 4.7 copy-start
  352.1 254.7 %collective-permute-start = (bf16[128,2048]{1,0:T(8,128)(2,1)S(1)}, bf16[128,2048]{1,0:T(8,128)(2,1)}, u32[]{:S(2)}, u32[]{:S(2)}) collective-permute-start(bf16[128,2048]{1,0:T(8,128)(2,1)S(1)} %copy.59), channel_id=1, source_target_pairs={{0,64},{64,128},{128,192},{192,256},{256,320},{320,384},{384,448},... | collective-permute-start | bytes 1572872 | tf_op jit(solution)/shard_map/ppermute | solution.py:15
  508.3 4.0 copy-start.1
  518.6 4.7 copy-start.1
  530.8 4.7 copy-start.1
  543.1 4.7 copy-start.1
  555.3 4.7 copy-start.1
  567.5 4.7 copy-start.1
  579.8 4.7 copy-start.1
  592.0 4.7 copy-start.1
  601.7 19.8 %collective-permute-start.1 = (bf16[128,2048]{1,0:T(8,128)(2,1)S(1)}, bf16[128,2048]{1,0:T(8,128)(2,1)S(1)}, u32[]{:S(2)}, u32[]{:S(2)}) collective-permute-start(bf16[128,2048]{1,0:T(8,128)(2,1)S(1)} %copy.58), channel_id=1, source_target_pairs={{64,0},{128,64},{192,128},{256,192},{320,256},{384,320},{448,384},... | collective-permute-start | bytes 1572872 | tf_op jit(solution)/shard_map/ppermute | solution.py:15
Sparse Core Ops, SparseCore 0:
  14.7 232.6 all-gather.4
  249.5 247.0 all-gather.2
where the time goes:
time: 631 us; the launch traced here: 629 us
  blocking collectives  245 us (39%)
  waiting for transfers between devices  133 us (21%)
  matrix products  96.7 us (15%)
  other arithmetic  81.3 us (13%)
  local copies, waits for them, and re-layouts  40.2 us (6%)
  starting transfers between devices  16.8 us (3%)
  between operations  16.1 us (3%)
    all_gather x2, blocking collectives, local(): lax.all_gather(key_docs[stream_num:stream_num + 1], 'ctx', axis=2, tiled=...  241 us
    all_gather x2, waiting for transfers between devices, local(): lax.all_gather(head_major[stream_num:stream_num + 1], 'ctx', axis=2, tile...  120 us
    reduce_sum x16, other arithmetic, one_block(): row_sum = factor * row_sum + jnp.sum(exp_terms, axis=-1)  53.4 us
    dot_general x16, matrix products, one_block(): jnp.einsum('tgjn,ngd->tgjd', weights, value_rows, preferred_element_type=...  52.3 us
    dot_general x16, matrix products, one_block(): jnp.einsum('tgjd,ngd->tgjn', query_heads, key_rows, preferred_element_typ...  44.4 us
    add x16, other arithmetic, one_block(): row_sum = factor * row_sum + jnp.sum(exp_terms, axis=-1)  19.6 us
    slice x16, local copies, waits for them, and re-layouts, one_block(): value_rows = slab_piece[1].reshape(block_len, -1, HD)  17.2 us
    ppermute x2, starting transfers between devices, from_behind(): return lax.ppermute(block, axis, route)  16.7 us
  transfers between devices with their start and end apart: 4, of which 3 were waited for; matrix products, arithmetic and copies ran while one was open for 34% of the time, Pallas kernels for 0%

commit v1 on v0

--- a/solution.py
+++ b/solution.py
@@ -99,6 +99,13 @@
     finals = []
     for stream_num in range(2):
         fold_piece = make_fold([stream_num], query_list, doc_list, query_pos, query_end)
+
+        def replace_point(inputs, device_axis):
+            h_now = jnp.stack([inputs] * lax.psum(1, device_axis), axis=0)
+            newest = lax.all_to_all(h_now, device_axis, 0, 0)
+            work_now = jnp.concatenate(newest, axis=2)
+            return work_now
+
         result = fold_piece(
             (
                 (
@@ -108,7 +115,7 @@
                 ),
             ),
             (
-                lax.all_gather(head_major[stream_num : stream_num + 1], "ctx", axis=2, tiled=True),
+                replace_point(head_major[stream_num : stream_num + 1], "ctx"),
                 lax.all_gather(key_docs[stream_num : stream_num + 1], "ctx", axis=2, tiled=True),
             ),
             jnp.int32(0),

time: 631 us -> 848 us (1.34)
  the two profiles are of different devices: /device:TPU:2 before, /device:TPU:4 now
where the time goes in v1:
time: 848 us; the launch traced here: 846 us
  blocking collectives  367 us (43%)
  waiting for transfers between devices  200 us (24%)
  matrix products  96.8 us (11%)
  other arithmetic  81.2 us (10%)
  local copies, waits for them, and re-layouts  60.5 us (7%)
  starting transfers between devices  36.4 us (4%)
    all_gather x2, blocking collectives, local(): lax.all_gather(key_docs[stream_num:stream_num + 1], 'ctx', axis=2, tiled=...  363 us
    all_to_all x2, waiting for transfers between devices, replace_point(): newest = lax.all_to_all(h_now, device_axis, 0, 0)  188 us
    reduce_sum x16, other arithmetic, one_block(): row_sum = factor * row_sum + jnp.sum(exp_terms, axis=-1)  53.3 us
    dot_general x16, matrix products, one_block(): jnp.einsum('tgjn,ngd->tgjd', weights, value_rows, preferred_element_type=...  52.2 us
    dot_general x16, matrix products, one_block(): jnp.einsum('tgjd,ngd->tgjn', query_heads, key_rows, preferred_element_typ...  44.6 us
    all_to_all x2, starting transfers between devices, replace_point(): newest = lax.all_to_all(h_now, device_axis, 0, 0)  21.3 us
    add x16, other arithmetic, one_block(): row_sum = factor * row_sum + jnp.sum(exp_terms, axis=-1)  19.6 us
    slice x16, local copies, waits for them, and re-layouts, one_block(): value_rows = slab_piece[1].reshape(block_len, -1, HD)  17.2 us
  transfers between devices with their start and end apart: 4, of which 2 were waited for; matrix products, arithmetic and copies ran while one was open for 27% of the time, Pallas kernels for 0%

profile of v1, /device:TPU:4, one launch (start us, length us, event | category | flops | bytes accessed | tf_op | source)
XLA Modules:
  0.0 845.7 jit_solution(10653444338810622211)
XLA Ops:
  2.0 3.9 all_to_all.25
  7.4 3.0 stack.17
  10.4 15.7 %all-to-all-start.2 = ((bf16[32,1,2,128,256]{3,4,2,1,0:T(8,128)(2,1)}), bf16[32,1,2,128,256]{3,4,2,1,0:T(8,128)(2,1)}, u32[]{:S(2)}, u32[]{:S(2)}) async-start(bf16[32,1,2,128,256]{3,4,2,1,0:T(8,128)(2,1)} %stack.17), calls=%async_computation.2 | async-start | bytes 8388608 | tf_op jit(solution)/shard_map/all_to_all | solution.py:105
  26.2 188.5 %all-to-all-done.2 = bf16[32,1,2,128,256]{3,4,2,1,0:T(8,128)(2,1)} async-done(((bf16[32,1,2,128,256]{3,4,2,1,0:T(8,128)(2,1)}), bf16[32,1,2,128,256]{3,4,2,1,0:T(8,128)(2,1)}, u32[]{:S(2)}, u32[]{:S(2)}) %all-to-all-start.2) | async-done | bytes 4194336 | tf_op jit(solution)/shard_map/all_to_all | solution.py:105
  214.7 3.0 stack.15
  217.7 5.7 all-to-all-start.1
  223.4 228.3 %all_gather.7 = s32[1,1,4096]{2,1,0:T(1,128)S(1)} all-gather(s32[1,1,128]{2,1,0:T(1,128)S(1)} %get-tuple-element.558), channel_id=1, replica_groups=mesh['section'=8,'ctx'=32,'tp'=2] {'ctx'}, dimensions={2}, use_global_device_ids=true | all-gather | bytes 16896 | tf_op jit(solution)/shard_map/all_gather | solution.py:119
  454.2 111.0 %conditional.3 = (f32[128,2,8]{0,2,1:T(8,128)}, f32[128,2,8,128]{0,3,2,1:T(8,128)}) conditional(s32[]{:T(128)} %convert_element_type.35, () %tuple.51, (bf16[1,2,32,128,256]{3,4,1,0,2:T(8,128)(2,1)}, s32[1,1,4096]{2,1,0:T(1,128)S(1)}, bf16[1,2,128,2048]{3,2,1,0:T(8,128)(2,1)S(1)}, s32[1,1,128]{2,1,0:T(1,128)S(1)}, s32[128]{0:T(128)S(1)}) %tuple.120), branch_computations={%region_6.7_spmd, %region_7.12_spmd} | conditional | flops 551496192 | bytes 54930812 | solution.py:59
  454.2 6.8 copy.51
  461.0 7.3 squeeze_reshape.7
  469.4 95.9 %while.35 = (s32[]{:T(128)}, f32[128,2,8]{0,2,1:T(8,128)S(1)}, f32[128,2,8]{0,2,1:T(8,128)}, f32[128,2,8,128]{0,3,2,1:T(8,128)}, s32[1,1,128]{2,1,0:T(1,128)S(1)...) while((s32[]{:T(128)}, f32[128,2,8]{0,2,1:T(8,128)S(1)}, ...), condition=%wide.region_11.11_spmd.clone, body=%wide.region_8.10_spmd.clone.sunk | while | flops 551496192 | bytes 33959156 | solution.py:56
  473.5 3.3 fusion.62
  481.1 2.8 fusion.61
  483.8 3.3 fusion.62
  488.5 3.4 fusion.64
  493.3 2.8 fusion.61
  496.1 3.3 fusion.62
  500.7 3.4 fusion.64
  505.5 2.8 fusion.61
  508.3 3.3 fusion.62
  512.9 3.4 fusion.64
  517.7 2.8 fusion.61
  520.5 3.3 fusion.62
  525.2 3.4 fusion.64
  529.9 2.8 fusion.61
  532.7 3.3 fusion.62
  537.4 3.4 fusion.64
  542.2 2.8 fusion.61
  544.9 3.3 fusion.62
  549.6 3.4 fusion.64
  554.4 2.8 fusion.61
  557.2 3.3 fusion.62
  561.8 3.4 fusion.64
  566.8 8.2 collective-permute-start
  575.0 134.7 %all_gather.6 = s32[1,1,4096]{2,1,0:T(1,128)S(1)} all-gather(s32[1,1,128]{2,1,0:T(1,128)S(1)} %get-tuple-element.557), channel_id=1, replica_groups=mesh['section'=8,'ctx'=32,'tp'=2] {'ctx'}, dimensions={2}, use_global_device_ids=true | all-gather | bytes 16896 | tf_op jit(solution)/shard_map/all_gather | solution.py:119
  711.7 111.5 %conditional.2 = (f32[128,2,8]{0,2,1:T(8,128)}, f32[128,2,8,128]{0,3,2,1:T(8,128)}) conditional(s32[]{:T(128)} %convert_element_type.32, () %tuple.49, (bf16[1,2,32,128,256]{3,4,1,0,2:T(8,128)(2,1)}, s32[1,1,4096]{2,1,0:T(1,128)S(1)}, bf16[1,2,128,2048]{3,2,1,0:T(8,128)(2,1)S(1)}, s32[1,1,128]{2,1,0:T(1,128)S(1)}, s32[128]{0:T(128)S(1)}) %tuple.121), branch_computations={%region_0.0_spmd, %region_1.6_spmd} | conditional | flops 551496192 | bytes 54930812 | solution.py:59
  711.9 6.9 copy.46
  718.7 7.4 squeeze_reshape.6
  727.1 96.1 %while.34 = (s32[]{:T(128)}, f32[128,2,8]{0,2,1:T(8,128)S(1)}, f32[128,2,8]{0,2,1:T(8,128)}, f32[128,2,8,128]{0,3,2,1:T(8,128)}, s32[1,1,128]{2,1,0:T(1,128)S(1)...) while((s32[]{:T(128)}, f32[128,2,8]{0,2,1:T(8,128)S(1)}, ...), condition=%wide.region_5.5_spmd.clone, body=%wide.region_2.4_spmd.clone.sunk | while | flops 551496192 | bytes 33959156 | solution.py:56
  728.5 2.8 fusion.69
  731.3 3.3 fusion.70
  738.8 2.8 fusion.69
  741.7 3.3 fusion.70
  746.3 3.4 fusion.72
  751.1 2.8 fusion.69
  753.9 3.3 fusion.70
  758.5 3.4 fusion.72
  763.3 2.8 fusion.69
  766.1 3.3 fusion.70
  770.8 3.4 fusion.72
  775.6 2.8 fusion.69
  778.4 3.3 fusion.70
  783.0 3.4 fusion.72
  787.8 2.8 fusion.69
  790.6 3.3 fusion.70
  795.3 3.4 fusion.72
  800.1 2.8 fusion.69
  802.9 3.3 fusion.70
  807.5 3.4 fusion.72
  812.3 2.8 fusion.69
  815.1 3.3 fusion.70
  819.8 3.4 fusion.72
  824.8 6.9 collective-permute-start.1
  832.8 11.8 %collective-permute-done.1 = bf16[128,2048]{1,0:T(8,128)(2,1)S(1)} collective-permute-done((bf16[128,2048]{1,0:T(8,128)(2,1)S(1)}, bf16[128,2048]{1,0:T(8,128)(2,1)S(1)}, u32[]{:S(2)}, u32[]{:S(2)}) %collective-permute-start.1) | collective-permute-done | bytes 524320 | tf_op jit(solution)/shard_map/ppermute | solution.py:15
  (187 shorter events, 61.2 us)
Async XLA Ops:
  10.4 204.3 %all-to-all-start.2 = ((bf16[32,1,2,128,256]{3,4,2,1,0:T(8,128)(2,1)}), bf16[32,1,2,128,256]{3,4,2,1,0:T(8,128)(2,1)}, u32[]{:S(2)}, u32[]{:S(2)}) async-start(bf16[32,1,2,128,256]{3,4,2,1,0:T(8,128)(2,1)} %stack.17), calls=%async_computation.2 | async-start | bytes 8388608 | tf_op jit(solution)/shard_map/all_to_all | solution.py:105
  217.7 5.7 copy-start.3
  217.7 236.5 %copy-start.2 = (bf16[1,2,128,2048]{3,2,1,0:T(8,128)(2,1)S(1)}, bf16[1,2,128,2048]{3,2,1,0:T(8,128)(2,1)}, u32[]{:S(2)}) copy-start(bf16[1,2,128,2048]{3,2,1,0:T(8,128)(2,1)} %param.11) | copy-start | bytes 3145732
  217.7 494.0 %all-to-all-start.1 = ((bf16[32,1,2,128,256]{3,4,2,1,0:T(8,128)(2,1)}), bf16[32,1,2,128,256]{3,4,2,1,0:T(8,128)(2,1)}, u32[]{:S(2)}, u32[]{:S(2)}) async-start(bf16[32,1,2,128,256]{3,4,2,1,0:T(8,128)(2,1)} %stack.15), calls=%async_computation.1 | async-start | bytes 8388608 | tf_op jit(solution)/shard_map/all_to_all | solution.py:105
  473.5 4.0 copy-start
  483.8 4.7 copy-start
  496.1 4.7 copy-start
  508.3 4.7 copy-start
  520.5 4.7 copy-start
  532.7 4.7 copy-start
  544.9 4.7 copy-start
  557.1 4.7 copy-start
  566.8 264.9 %collective-permute-start = (bf16[128,2048]{1,0:T(8,128)(2,1)S(1)}, bf16[128,2048]{1,0:T(8,128)(2,1)}, u32[]{:S(2)}, u32[]{:S(2)}) collective-permute-start(bf16[128,2048]{1,0:T(8,128)(2,1)S(1)} %copy.62), channel_id=1, source_target_pairs={{0,64},{64,128},{128,192},{192,256},{256,320},{320,384},{384,448},... | collective-permute-start | bytes 1572872 | tf_op jit(solution)/shard_map/ppermute | solution.py:15
  731.3 4.0 copy-start.1
  741.6 4.7 copy-start.1
  753.9 4.7 copy-start.1
  766.1 4.7 copy-start.1
  778.4 4.7 copy-start.1
  790.6 4.7 copy-start.1
  802.9 4.7 copy-start.1
  815.1 4.7 copy-start.1
  824.8 19.8 %collective-permute-start.1 = (bf16[128,2048]{1,0:T(8,128)(2,1)S(1)}, bf16[128,2048]{1,0:T(8,128)(2,1)S(1)}, u32[]{:S(2)}, u32[]{:S(2)}) collective-permute-start(bf16[128,2048]{1,0:T(8,128)(2,1)S(1)} %copy.61), channel_id=1, source_target_pairs={{64,0},{128,64},{192,128},{256,192},{320,256},{384,320},{448,384},... | collective-permute-start | bytes 1572872 | tf_op jit(solution)/shard_map/ppermute | solution.py:15
